TPU v7x, 128 devices: a whole 4x4x4 slice. The times are simulated.
128 devices in a mesh: rep: 16 (over x, y), exp: 8 (over z, core).
Axes of the slice: x: 4, y: 4, z: 4, core: 2. Of those that a mesh axis runs over, the one named last changes fastest.
Arguments:
- hidden: bfloat16 [16384, 4096], P(('rep', 'exp')), may hold values from -6 to 6
- parents: int32 [16384], P(('rep', 'exp')), may hold values from 0 to 1023
- routes: int32 [16384, 8], P(('rep', 'exp')), may hold values from 0 to 127, all different within a row; in each aligned block of 128 rows (0 to 127, 128 to 255, ...) at most 10 rows name the same one
- gates: float32 [16384, 8], P(('rep', 'exp')), may hold values from 0.05 to 1
- counts: int32 [128], P(('rep', 'exp')), may hold values from 64 to 128, as said below
- norm_gain: float32 [4096], replicated, may hold values from 0.1 to 1.9
- w_gate: bfloat16 [128, 4096, 768], P(('rep', 'exp')), may hold values from -0.09375 to 0.09375
- w_up: bfloat16 [128, 4096, 768], P(('rep', 'exp')), may hold values from -0.09375 to 0.09375
- w_down: bfloat16 [128, 768, 4096], P(('rep', 'exp')), may hold values from -0.21875 to 0.21875
Outputs:
- mixed: bfloat16 [16384, 4096], P(('rep', 'exp'))
Inputs may be any that keep to these rules, and one draw needn't show every extreme that they name: `routes`: in the rows of one device no expert is named more than 10 times. `counts`: some device has all of its rows live.
All inputs are finite; a program needn't handle non-finite values.
Results may differ from a plain program's by a relative error of at most 0.0071.
Values may be sent and summed in bfloat16 or wider, within the bound.
A program may use at most 128 MiB of HBM per device.

v0:
```python
import jax
import jax.numpy as jnp
from jax import lax
from jax.sharding import PartitionSpec as P


def run_expert(arrived, w_gate, w_up, w_down):
    gate_val = jnp.dot(arrived, w_gate[0], preferred_element_type=jnp.float32)
    up_val = jnp.dot(arrived, w_up[0], preferred_element_type=jnp.float32)
    act = (jax.nn.silu(gate_val) * up_val).astype(jnp.bfloat16)
    return jnp.dot(act, w_down[0], preferred_element_type=jnp.float32).astype(jnp.bfloat16)


def shards(hidden, parents, routes, gates, counts, norm_gain, w_gate, w_up, w_down):
    rows = hidden.shape[0]
    width = hidden.shape[1]
    top = routes.shape[1]
    n_rep = lax.axis_size("rep")
    n_exp = lax.axis_size("exp")
    n_dev = n_rep * n_exp
    cap = rows * top // n_dev + 2
    column = lax.axis_index("exp")
    micro = rows * n_exp
    per_expert = cap * n_exp
    slots = n_rep * per_expert
    live = jnp.arange(rows, dtype=jnp.int32) < counts[0]
    weights = gates / jnp.sum(gates, axis=1, keepdims=True) * live[:, None].astype(jnp.float32)
    flat = routes.reshape(-1)
    live_slot = jnp.repeat(live, top)
    onehot = (
        (flat[:, None] == jnp.arange(n_dev, dtype=jnp.int32)[None, :]) & live_slot[:, None]
    ).astype(jnp.int32)
    before = jnp.cumsum(onehot, axis=0) - onehot
    rank = jnp.sum(before * onehot, axis=1)
    code = jnp.where(live_slot, flat, -1)
    ints = jnp.concatenate(
        [code.reshape(rows, top), rank.reshape(rows, top), parents[:, None]], axis=1
    )
    group = lax.all_gather(hidden, "exp", axis=0, tiled=True)
    ints_all = lax.all_gather(ints, "exp", axis=0, tiled=True)
    w_all = lax.all_gather(weights, "exp", axis=0, tiled=True)
    code_all = ints_all[:, :top]
    rank_all = ints_all[:, top : 2 * top]
    parent_all = ints_all[:, 2 * top]
    mine = (code_all >= 0) & (code_all % n_exp == column)
    owner = (jnp.arange(micro, dtype=jnp.int32) // rows)[:, None]
    dest = code_all // n_exp * per_expert + owner * cap + rank_all
    dest = jnp.where(mine, dest, slots).reshape(-1)
    row_id = jnp.broadcast_to(jnp.arange(micro, dtype=jnp.int32)[:, None], (micro, top)).reshape(-1)
    src_row = jnp.zeros((slots,), jnp.int32).at[dest].set(row_id, mode="drop")
    filled = jnp.zeros((slots,), jnp.bool_).at[dest].set(True, mode="drop")
    slot_w = jnp.zeros((slots,), jnp.float32).at[dest].set(w_all.reshape(-1), mode="drop")
    picked = jnp.take(group, jnp.take(parent_all, src_row), axis=0).astype(jnp.float32)
    scale = lax.rsqrt(jnp.mean(picked * picked, axis=1, keepdims=True) + 1e-06)
    normed = (picked * scale * norm_gain).astype(jnp.bfloat16)
    outgoing = jnp.where(filled[:, None], normed, jnp.zeros((), jnp.bfloat16))
    arrived = lax.all_to_all(outgoing, "rep", split_axis=0, concat_axis=0, tiled=True)
    results = run_expert(arrived, w_gate, w_up, w_down)
    returned = lax.all_to_all(results, "rep", split_axis=0, concat_axis=0, tiled=True)
    contrib = slot_w[:, None] * returned.astype(jnp.float32)
    target = jnp.where(filled, src_row, micro)
    partial = jnp.zeros((micro, width), jnp.float32).at[target].add(contrib, mode="drop")
    mixed = lax.psum_scatter(partial.astype(jnp.bfloat16), "exp", scatter_dimension=0, tiled=True)
    return mixed


def solution(mesh):
    placed = (
        P(("rep", "exp"), None),
        P(("rep", "exp")),
        P(("rep", "exp"), None),
        P(("rep", "exp"), None),
        P(("rep", "exp")),
        P(),
        P(("rep", "exp"), None, None),
        P(("rep", "exp"), None, None),
        P(("rep", "exp"), None, None),
    )
    return jax.shard_map(
        shards, mesh=mesh, in_specs=placed, out_specs=P(("rep", "exp"), None), check_vma=False
    )
```

profile of v0, /device:TPU:1, one launch (start us, length us, event | category | flops | bytes accessed | tf_op | source)
XLA Modules:
  0.0 590.4 jit_solution(2126128571061677138)
XLA Ops:
  6.5 0.7 all-gather.2.cloned.1.call-update
  7.3 0.8 copy.28
  9.2 0.3 fusion.17
  9.8 0.5 fusion.16
  10.4 0.7 broadcast_select_fusion
  11.1 0.7 pad_add_fusion
  11.8 15.3 %all_gather.9 = s32[1024,17]{0,1:T(8,128)S(1)} all-gather(s32[128,17]{0,1:T(8,128)S(1)} %pad_add_fusion), channel_id=1, replica_groups=mesh['rep'=16,'exp'=8] {'exp'}, dimensions={0}, use_global_device_ids=true | all-gather | bytes 78336 | tf_op jit(solution)/shard_map/all_gather | solution.py:40
  27.7 34.6 %scatter_custom_fusion = pred[1280]{0:T(1024)(128)(4,1)S(1)} fusion(s32[8192]{0:T(1024)S(1)} %bitcast.48, pred[8192]{0:T(1024)(128)(4,1)S(1)} %broadcast.149, pred[]{:T(512)} %constant.90.clone.1), kind=kCustom, calls=%fused_computation.72 | custom fusion | bytes 1281 | tf_op jit(solution)/shard_map/scatter | solution.py:51
  62.7 30.9 %scatter_custom_fusion.1 = s32[1280]{0:T(1024)S(1)} fusion(s32[8192]{0:T(1024)S(1)} %bitcast.49, s32[8192]{0:T(1024)S(1)} %reshape.182, s32[]{:T(128)} %constant.93.clone.1), kind=kCustom, calls=%fused_computation.69 | custom fusion | bytes 5124 | tf_op jit(solution)/shard_map/scatter | solution.py:50
  93.6 5.0 gather_fusion
  98.7 23.2 %gather_fusion.1 = bf16[1280,4096]{1,0:T(8,128)(2,1)} fusion(bf16[1024,4096]{1,0:T(8,128)(2,1)} %all-gather.2.cloned.1.call-done, s32[2048]{0:T(1024)S(1)} %pad_clamp_fusion), kind=kCustom, calls=%fused_computation.1 | custom fusion | bytes 20976640 | tf_op jit(solution)/shard_map/jit(_take)/gather | solution.py:53
  121.9 6.9 %multiply_reduce_fusion = f32[1280]{0:T(1024)S(1)} fusion(bf16[1280,4096]{1,0:T(8,128)(2,1)} %gather_fusion.1, pred[1280]{0:T(1024)(128)(4,1)S(1)} %get-tuple-element.5), kind=kLoop, calls=%fused_computation.9 | loop fusion | flops 20970240 | bytes 10492160 | tf_op jit(solution)/shard_map/reduce_sum | solution.py:54
  128.9 9.0 %fusion.1 = bf16[16,80,4096]{2,1,0:T(8,128)(2,1)S(1)} fusion(f32[4096]{0:T(1024)S(1)} %copy-done, f32[16,80]{1,0:T(8,128)S(1)} %rsqrt.12, bf16[16,80,4096]{2,1,0:T(8,128)(2,1)} %bitcast.44, pred[16,80]{1,0:T(8,128)(4,1)S(1)} %broadcast_in_dim.109, pred[16,80]{1,0:T(8,128)(4,1)S(1)} %broadcast_in_dim.105), kind=kLoop, calls=%fused_computation.11 | loop fusion | flops 31457280 | bytes 20995584 | tf_op jit(solution)/shard_map/jit(_where)/select_n | solution.py:56
  138.0 123.9 %all_to_all.18 = bf16[16,80,4096]{2,1,0:T(8,128)(2,1)S(1)} all-to-all(bf16[16,80,4096]{2,1,0:T(8,128)(2,1)S(1)} %fusion.1), channel_id=1, replica_groups=mesh['rep'=16,'exp'=8] {'rep'}, dimensions={0} | all-to-all | bytes 20971520 | tf_op jit(solution)/shard_map/all_to_all | solution.py:57
  261.9 11.8 %fusion.7 = f32[1280,768]{1,0:T(8,128)} fusion(bf16[1280,4096]{1,0:T(8,128)(2,1)S(1)} %bitcast.46, bf16[1,4096,768]{2,1,0:T(8,128)(2,1)} %param.15), kind=kOutput, calls=%fused_computation.17 | convolution fusion | flops 8053063680 | bytes 20709376 | tf_op jit(solution)/shard_map/dot_general | solution.py:8
  273.7 10.3 %fusion.12 = bf16[1280,768]{1,0:T(8,128)(2,1)S(1)} fusion(bf16[1280,4096]{1,0:T(8,128)(2,1)S(1)} %bitcast.47, bf16[1,4096,768]{2,1,0:T(8,128)(2,1)S(1)} %bitcast.53, f32[1280,768]{1,0:T(8,128)} %fusion.7), kind=kOutput, calls=%fused_computation.20 | convolution fusion | flops 8058961920 | bytes 22675456 | tf_op jit(solution)/shard_map/dot_general | solution.py:9
  284.1 10.7 %convolution_convert_fusion = bf16[1280,4096]{1,0:T(8,128)(2,1)} fusion(bf16[1280,768]{1,0:T(8,128)(2,1)S(1)} %fusion.12, bf16[1,768,4096]{2,1,0:T(8,128)(2,1)S(1)} %bitcast.55), kind=kOutput, calls=%fused_computation.10 | convolution fusion | flops 8058306560 | bytes 18743296 | tf_op jit(solution)/shard_map/dot_general | solution.py:11
  294.7 5.0 all-to-all-start.1
  299.8 14.9 %all_gather.10 = f32[1024,8]{0,1:T(8,128)S(1)} all-gather(f32[128,8]{0,1:T(8,128)S(1)} %divide_multiply_fusion), channel_id=1, replica_groups=mesh['rep'=16,'exp'=8] {'exp'}, dimensions={0}, use_global_device_ids=true | all-gather | bytes 36864 | tf_op jit(solution)/shard_map/all_gather | solution.py:41
  315.1 30.4 %scatter_custom_fusion.2 = f32[1280]{0:T(1024)S(1)} fusion(s32[8192]{0:T(1024)S(1)} %bitcast.50, f32[8192]{0:T(1024)S(1)} %reshape.190, f32[]{:T(128)} %constant.89.clone.1), kind=kCustom, calls=%fused_computation.67 | custom fusion | bytes 5124 | tf_op jit(solution)/shard_map/scatter | solution.py:52
  345.6 126.3 %all-to-all-done.1 = bf16[16,80,4096]{2,1,0:T(8,128)(2,1)} async-done(((bf16[16,80,4096]{2,1,0:T(8,128)(2,1)}), bf16[16,80,4096]{2,1,0:T(8,128)(2,1)}, u32[]{:S(2)}, u32[]{:S(2)}) %all-to-all-start.1) | async-done | bytes 10485792 | tf_op jit(solution)/shard_map/all_to_all | solution.py:59
  471.9 42.9 %scatter_custom_fusion.3 = f32[1024,4096]{1,0:T(8,128)} fusion(s32[1280]{0:T(1024)S(1)} %get-tuple-element.8, bf16[1280,4096]{1,0:T(8,128)(2,1)} %bitcast.16, f32[1280]{0:T(1024)S(1)} %scatter_custom_fusion.2, f32[]{:T(128)} %constant.89.clone.1), kind=kCustom, calls=%fused_computation.7 | custom fusion | flops 15728640 | bytes 27271172 | tf_op jit(solution)/shard_map/scatter-add | solution.py:62
  514.8 9.0 %convert_element_type.50 = bf16[1024,4096]{1,0:T(8,128)(2,1)} convert(f32[1024,4096]{1,0:T(8,128)} %scatter_custom_fusion.3) | non-fusion elementwise | flops 4194304 | bytes 25165824 | tf_op jit(solution)/shard_map/convert_element_type | solution.py:63
  523.8 59.5 %reduce-scatter.2.cloned.1.call-done = bf16[128,4096]{1,0:T(8,128)(2,1)} async-done(((bf16[1024,4096]{1,0:T(8,128)(2,1)}), bf16[128,4096]{1,0:T(8,128)(2,1)}) %reduce-scatter.2.cloned.1.call-update) | async-done | bytes 1048592 | tf_op jit(solution)/shard_map/reduce_scatter | solution.py:63
  (55 shorter events, 2.5 us)
Async XLA Ops:
  6.5 92.2 %all-gather.2.cloned.1.call-start = ((), (), s32[]{:S(2)}) async-start(), calls=%async_computation.3 | async-start | bytes 9437184 | tf_op jit(solution)/shard_map/all_gather | solution.py:39
  121.9 7.0 %copy-start = (f32[4096]{0:T(1024)S(1)}, f32[4096]{0:T(1024)}, u32[]{:S(2)}) copy-start(f32[4096]{0:T(1024)} %param.14) | copy-start | bytes 49156
  138.0 135.8 %slice-start = ((s8[6291456]{0:T(1024)(128)(4,1)}), s8[4194304]{0:T(1024)(128)(4,1)S(1)}, s32[]{:S(2)}) async-start(s8[6291456]{0:T(1024)(128)(4,1)} %bitcast.52), calls=%async_computation.5 | async-start | bytes 8388608
  138.0 146.1 %slice-start.2 = ((s8[6291456]{0:T(1024)(128)(4,1)}), s8[4194304]{0:T(1024)(128)(4,1)S(1)}, s32[]{:S(2)}) async-start(s8[6291456]{0:T(1024)(128)(4,1)} %bitcast.54), calls=%async_computation.7 | async-start | bytes 8388608
  261.9 11.8 %slice-start.1 = ((s8[6291456]{0:T(1024)(128)(4,1)}), s8[2097152]{0:T(1024)(128)(4,1)S(1)}, s32[]{:S(2)}) async-start(s8[6291456]{0:T(1024)(128)(4,1)} %bitcast.52), calls=%async_computation.6 | async-start | bytes 4194304
  261.9 22.2 %slice-start.3 = ((s8[6291456]{0:T(1024)(128)(4,1)}), s8[2097152]{0:T(1024)(128)(4,1)S(1)}, s32[]{:S(2)}) async-start(s8[6291456]{0:T(1024)(128)(4,1)} %bitcast.54), calls=%async_computation.8 | async-start | bytes 4194304
  294.7 5.0 copy-start.1
  294.7 177.1 %all-to-all-start.1 = ((bf16[16,80,4096]{2,1,0:T(8,128)(2,1)}), bf16[16,80,4096]{2,1,0:T(8,128)(2,1)}, u32[]{:S(2)}, u32[]{:S(2)}) async-start(bf16[16,80,4096]{2,1,0:T(8,128)(2,1)} %bitcast.45), calls=%async_computation.1 | async-start | bytes 20971520 | tf_op jit(solution)/shard_map/all_to_all | solution.py:59
  299.7 283.6 %reduce-scatter.2.cloned.1.call-start = ((), (), s32[]{:S(2)}) async-start(), calls=%async_computation.4 | async-start | bytes 9437184 | tf_op jit(solution)/shard_map/reduce_scatter | solution.py:63
Sparse Core Ops, SparseCore 0:
  9.1 53.5 all-gather.1
  523.9 59.3 reduce-scatter.1
where the time goes:
time: 597 us; the launch traced here: 590 us
  waiting for transfers between devices  187 us (31%)
  blocking collectives  154 us (26%)
  local copies, waits for them, and re-layouts  127 us (21%)
  other arithmetic  70.3 us (12%)
  matrix products  32.8 us (5%)
  between operations  14.6 us (2%)
    all_to_all x1, waiting for transfers between devices, shards(): lax.all_to_all(results, 'rep', split_axis=0, concat_axis=0, tiled=True)  126 us
    all_to_all x1, blocking collectives, shards(): lax.all_to_all(outgoing, 'rep', split_axis=0, concat_axis=0, tiled=True)  124 us
    reduce_scatter x1, waiting for transfers between devices, shards(): lax.psum_scatter(partial.astype(jnp.bfloat16), 'exp', scatter_dimension=0...  59.5 us
    scatter-add x1, other arithmetic, shards(): jnp.zeros((micro, width), jnp.float32).at[target].add(contrib, mode='drop')  42.9 us
    scatter x1, local copies, waits for them, and re-layouts, shards(): filled = jnp.zeros((slots,), jnp.bool_).at[dest].set(True, mode='drop')  34.6 us
    scatter x1, local copies, waits for them, and re-layouts, shards(): src_row = jnp.zeros((slots,), jnp.int32).at[dest].set(row_id, mode='drop')  30.9 us
    scatter x1, local copies, waits for them, and re-layouts, shards(): jnp.zeros((slots,), jnp.float32).at[dest]  30.4 us
    gather x1, local copies, waits for them, and re-layouts, shards(): jnp.take(group, jnp.take(parent_all, src_row), axis=0).astype(jnp.float32)  23.2 us
  transfers between devices with their start and end apart: 3, of which 2 were waited for; matrix products, arithmetic and copies ran while one was open for 18% of the time, Pallas kernels for 0%

commit v1 on v0

--- a/solution.py
+++ b/solution.py
@@ -38,7 +38,10 @@
     )
     group = lax.all_gather(hidden, "exp", axis=0, tiled=True)
     ints_all = lax.all_gather(ints, "exp", axis=0, tiled=True)
-    w_all = lax.all_gather(weights, "exp", axis=0, tiled=True)
+    size = lax.axis_size("exp")
+    blocks = jnp.stack([weights for _ in range(size)])
+    blocks = lax.all_to_all(blocks, "exp", split_axis=0, concat_axis=0)
+    w_all = jnp.concatenate(blocks, axis=0)
     code_all = ints_all[:, :top]
     rank_all = ints_all[:, top : 2 * top]
     parent_all = ints_all[:, 2 * top]

time: 597 us -> 688 us (1.15)
  waiting for transfers between devices: 187 us -> 389 us
  blocking collectives: 154 us -> 15.3 us
  starting transfers between devices: 5.02 us -> 22.6 us
    all_to_all x0 -> x2, waiting for transfers between devices: none -> 180 us  [the longest x1 180 us: shards(): lax.all_to_all(outgoing, 'rep', split_axis=0, concat_axis=0, tiled=True)]
    all_to_all x1 -> x0, blocking collectives: 124 us -> none  [shards(): lax.all_to_all(outgoing, 'rep', split_axis=0, concat_axis=0, tiled=True)]
    all_to_all x1, waiting for transfers between devices: 126 us -> 151 us  [shards(): lax.all_to_all(results, 'rep', split_axis=0, concat_axis=0, tiled=True)]
    all_gather x1 -> x0, blocking collectives: 14.9 us -> none  [shards(): w_all = lax.all_gather(weights, 'exp', axis=0, tiled=True)]
    all_to_all x0 -> x2, starting transfers between devices: none -> 12.2 us  [the longest x1 6.93 us: shards(): lax.all_to_all(outgoing, 'rep', split_axis=0, concat_axis=0, tiled=True)]
  transfers between devices with their start and end apart: 3 -> 5, of which waited for: 2 -> 3; matrix products, arithmetic and copies ran while one was open for 18% -> 21% of each run, Pallas kernels for 0% -> 0%
where the time goes in v1:
time: 688 us; the launch traced here: 681 us
  waiting for transfers between devices  389 us (57%)
  local copies, waits for them, and re-layouts  128 us (19%)
  other arithmetic  73.1 us (11%)
  matrix products  38.8 us (6%)
  starting transfers between devices  22.6 us (3%)
  blocking collectives  15.3 us (2%)
  between operations  14.5 us (2%)
    all_to_all x1, waiting for transfers between devices, shards(): lax.all_to_all(outgoing, 'rep', split_axis=0, concat_axis=0, tiled=True)  180 us
    all_to_all x1, waiting for transfers between devices, shards(): lax.all_to_all(results, 'rep', split_axis=0, concat_axis=0, tiled=True)  151 us
    reduce_scatter x1, waiting for transfers between devices, shards(): lax.psum_scatter(partial.astype(jnp.bfloat16), 'exp', scatter_dimension=0...  57.8 us
    scatter-add x1, other arithmetic, shards(): jnp.zeros((micro, width), jnp.float32).at[target].add(contrib, mode='drop')  42.9 us
    scatter x1, local copies, waits for them, and re-layouts, shards(): filled = jnp.zeros((slots,), jnp.bool_).at[dest].set(True, mode='drop')  34.6 us
    scatter x1, local copies, waits for them, and re-layouts, shards(): src_row = jnp.zeros((slots,), jnp.int32).at[dest].set(row_id, mode='drop')  30.9 us
    scatter x1, local copies, waits for them, and re-layouts, shards(): jnp.zeros((slots,), jnp.float32).at[dest]  30.4 us
    gather x1, local copies, waits for them, and re-layouts, shards(): jnp.take(group, jnp.take(parent_all, src_row), axis=0).astype(jnp.float32)  23.2 us
  transfers between devices with their start and end apart: 5, of which 3 were waited for; matrix products, arithmetic and copies ran while one was open for 21% of the time, Pallas kernels for 0%

profile of v1, /device:TPU:1, one launch (start us, length us, event | category | flops | bytes accessed | tf_op | source)
XLA Modules:
  0.0 680.9 jit_solution(4872146271243257777)
XLA Ops:
  6.5 0.7 all-gather.2.cloned.1.call-update
  7.3 0.8 copy.29
  10.4 0.7 broadcast_select_fusion
  11.1 0.7 pad_add_fusion
  11.8 15.3 %all_gather.6 = s32[1024,17]{0,1:T(8,128)S(1)} all-gather(s32[128,17]{0,1:T(8,128)S(1)} %pad_add_fusion), channel_id=1, replica_groups=mesh['rep'=16,'exp'=8] {'exp'}, dimensions={0}, use_global_device_ids=true | all-gather | bytes 78336 | tf_op jit(solution)/shard_map/all_gather | solution.py:40
  27.7 34.6 %scatter_custom_fusion = pred[1280]{0:T(1024)(128)(4,1)S(1)} fusion(s32[8192]{0:T(1024)S(1)} %bitcast.45, pred[8192]{0:T(1024)(128)(4,1)S(1)} %broadcast.151, pred[]{:T(512)} %constant.90.clone.1), kind=kCustom, calls=%fused_computation.72 | custom fusion | bytes 1281 | tf_op jit(solution)/shard_map/scatter | solution.py:54
  62.7 30.9 %scatter_custom_fusion.1 = s32[1280]{0:T(1024)S(1)} fusion(s32[8192]{0:T(1024)S(1)} %bitcast.46, s32[8192]{0:T(1024)S(1)} %reshape.180, s32[]{:T(128)} %constant.93.clone.1), kind=kCustom, calls=%fused_computation.69 | custom fusion | bytes 5124 | tf_op jit(solution)/shard_map/scatter | solution.py:53
  93.6 5.0 gather_fusion
  98.7 23.2 %gather_fusion.1 = bf16[1280,4096]{1,0:T(8,128)(2,1)} fusion(bf16[1024,4096]{1,0:T(8,128)(2,1)} %all-gather.2.cloned.1.call-done, s32[2048]{0:T(1024)S(1)} %pad_clamp_fusion), kind=kCustom, calls=%fused_computation.1 | custom fusion | bytes 20976640 | tf_op jit(solution)/shard_map/jit(_take)/gather | solution.py:56
  121.9 6.9 %multiply_reduce_fusion = f32[1280]{0:T(1024)S(1)} fusion(bf16[1280,4096]{1,0:T(8,128)(2,1)} %gather_fusion.1, pred[1280]{0:T(1024)(128)(4,1)S(1)} %get-tuple-element.5), kind=kLoop, calls=%fused_computation.9 | loop fusion | flops 20970240 | bytes 10492160 | tf_op jit(solution)/shard_map/reduce_sum | solution.py:57
  128.9 11.9 %fusion.1 = bf16[16,80,4096]{2,1,0:T(8,128)(2,1)} fusion(f32[4096]{0:T(1024)S(1)} %copy-done, f32[16,80]{1,0:T(8,128)S(1)} %rsqrt.12, bf16[16,80,4096]{2,1,0:T(8,128)(2,1)} %bitcast.43, pred[16,80]{1,0:T(8,128)(4,1)S(1)} %broadcast_in_dim.109, pred[16,80]{1,0:T(8,128)(4,1)S(1)} %broadcast_in_dim.105), kind=kLoop, calls=%fused_computation.11 | loop fusion | flops 31457280 | bytes 20995584 | tf_op jit(solution)/shard_map/jit(_where)/select_n | solution.py:59
  140.8 6.9 %all-to-all-start.1 = ((bf16[16,80,4096]{2,1,0:T(8,128)(2,1)}), bf16[16,80,4096]{2,1,0:T(8,128)(2,1)}, u32[]{:S(2)}, u32[]{:S(2)}) async-start(bf16[16,80,4096]{2,1,0:T(8,128)(2,1)} %fusion.1), calls=%async_computation.1 | async-start | bytes 20971520 | tf_op jit(solution)/shard_map/all_to_all | solution.py:60
  147.8 179.5 %all-to-all-done.1 = bf16[16,80,4096]{2,1,0:T(8,128)(2,1)} async-done(((bf16[16,80,4096]{2,1,0:T(8,128)(2,1)}), bf16[16,80,4096]{2,1,0:T(8,128)(2,1)}, u32[]{:S(2)}, u32[]{:S(2)}) %all-to-all-start.1) | async-done | bytes 10485792 | tf_op jit(solution)/shard_map/all_to_all | solution.py:60
  327.3 0.6 stack.2
  327.9 5.3 all-to-all-start
  333.2 12.1 %fusion.7 = f32[1280,768]{1,0:T(8,128)S(1)} fusion(bf16[1280,4096]{1,0:T(8,128)(2,1)} %bitcast.9, bf16[1,4096,768]{2,1,0:T(8,128)(2,1)} %param.15), kind=kOutput, calls=%fused_computation.17 | convolution fusion | flops 8053063680 | bytes 20709376 | tf_op jit(solution)/shard_map/dot_general | solution.py:8
  345.3 13.1 %fusion.12 = bf16[1280,768]{1,0:T(8,128)(2,1)S(1)} fusion(bf16[1280,4096]{1,0:T(8,128)(2,1)} %bitcast.9, bf16[1,4096,768]{2,1,0:T(8,128)(2,1)} %param.16, f32[1280,768]{1,0:T(8,128)S(1)} %fusion.7), kind=kOutput, calls=%fused_computation.20 | convolution fusion | flops 8058961920 | bytes 22675456 | tf_op jit(solution)/shard_map/dot_general | solution.py:9
  358.4 13.5 %convolution_convert_fusion = bf16[1280,4096]{1,0:T(8,128)(2,1)} fusion(bf16[1280,768]{1,0:T(8,128)(2,1)S(1)} %fusion.12, bf16[1,768,4096]{2,1,0:T(8,128)(2,1)} %param.17), kind=kOutput, calls=%fused_computation.10 | convolution fusion | flops 8058306560 | bytes 18743296 | tf_op jit(solution)/shard_map/dot_general | solution.py:11
  372.0 10.3 %all-to-all-start.2 = ((bf16[16,80,4096]{2,1,0:T(8,128)(2,1)}), bf16[16,80,4096]{2,1,0:T(8,128)(2,1)}, u32[]{:S(2)}, u32[]{:S(2)}) async-start(bf16[16,80,4096]{2,1,0:T(8,128)(2,1)} %bitcast.44), calls=%async_computation.2 | async-start | bytes 20971520 | tf_op jit(solution)/shard_map/all_to_all | solution.py:62
  382.8 30.4 %scatter_custom_fusion.2 = f32[1280]{0:T(1024)S(1)} fusion(s32[8192]{0:T(1024)S(1)} %bitcast.47, f32[8192]{0:T(1024)S(1)} %reshape.188, f32[]{:T(128)} %constant.89.clone.1), kind=kCustom, calls=%fused_computation.67 | custom fusion | bytes 5124 | tf_op jit(solution)/shard_map/scatter | solution.py:55
  413.3 150.8 %all-to-all-done.2 = bf16[16,80,4096]{2,1,0:T(8,128)(2,1)} async-done(((bf16[16,80,4096]{2,1,0:T(8,128)(2,1)}), bf16[16,80,4096]{2,1,0:T(8,128)(2,1)}, u32[]{:S(2)}, u32[]{:S(2)}) %all-to-all-start.2) | async-done | bytes 10485792 | tf_op jit(solution)/shard_map/all_to_all | solution.py:62
  564.1 42.9 %scatter_custom_fusion.3 = f32[1024,4096]{1,0:T(8,128)} fusion(s32[1280]{0:T(1024)S(1)} %get-tuple-element.8, bf16[1280,4096]{1,0:T(8,128)(2,1)} %bitcast.16, f32[1280]{0:T(1024)S(1)} %scatter_custom_fusion.2, f32[]{:T(128)} %constant.89.clone.1), kind=kCustom, calls=%fused_computation.7 | custom fusion | flops 15728640 | bytes 27271172 | tf_op jit(solution)/shard_map/scatter-add | solution.py:65
  606.9 9.0 %convert_element_type.50 = bf16[1024,4096]{1,0:T(8,128)(2,1)} convert(f32[1024,4096]{1,0:T(8,128)} %scatter_custom_fusion.3) | non-fusion elementwise | flops 4194304 | bytes 25165824 | tf_op jit(solution)/shard_map/convert_element_type | solution.py:66
  616.0 57.8 %reduce-scatter.2.cloned.1.call-done = bf16[128,4096]{1,0:T(8,128)(2,1)} async-done(((bf16[1024,4096]{1,0:T(8,128)(2,1)}), bf16[128,4096]{1,0:T(8,128)(2,1)}) %reduce-scatter.2.cloned.1.call-update) | async-done | bytes 1048592 | tf_op jit(solution)/shard_map/reduce_scatter | solution.py:66
  (47 shorter events, 3.4 us)
Async XLA Ops:
  6.5 92.2 %all-gather.2.cloned.1.call-start = ((), (), s32[]{:S(2)}) async-start(), calls=%async_computation.4 | async-start | bytes 9437184 | tf_op jit(solution)/shard_map/all_gather | solution.py:39
  121.9 7.0 %copy-start = (f32[4096]{0:T(1024)S(1)}, f32[4096]{0:T(1024)}, u32[]{:S(2)}) copy-start(f32[4096]{0:T(1024)} %param.14) | copy-start | bytes 49156
  140.8 6.9 %copy-start.1 = (f32[128,8]{0,1:T(8,128)S(1)}, f32[128,8]{0,1:T(8,128)}, u32[]{:S(2)}) copy-start(f32[128,8]{0,1:T(8,128)} %param.12) | copy-start | bytes 12292
  140.8 186.5 %all-to-all-start.1 = ((bf16[16,80,4096]{2,1,0:T(8,128)(2,1)}), bf16[16,80,4096]{2,1,0:T(8,128)(2,1)}, u32[]{:S(2)}, u32[]{:S(2)}) async-start(bf16[16,80,4096]{2,1,0:T(8,128)(2,1)} %fusion.1), calls=%async_computation.1 | async-start | bytes 20971520 | tf_op jit(solution)/shard_map/all_to_all | solution.py:60
  327.9 44.1 %all-to-all-start = ((f32[8,128,8]{1,2,0:T(8,128)}), f32[8,128,8]{1,2,0:T(8,128)S(1)}, u32[]{:S(2)}, u32[]{:S(2)}) async-start(f32[8,128,8]{1,2,0:T(8,128)} %stack.2), calls=%async_computation | async-start | bytes 65536 | tf_op jit(solution)/shard_map/all_to_all | solution.py:43
  372.0 192.1 %all-to-all-start.2 = ((bf16[16,80,4096]{2,1,0:T(8,128)(2,1)}), bf16[16,80,4096]{2,1,0:T(8,128)(2,1)}, u32[]{:S(2)}, u32[]{:S(2)}) async-start(bf16[16,80,4096]{2,1,0:T(8,128)(2,1)} %bitcast.44), calls=%async_computation.2 | async-start | bytes 20971520 | tf_op jit(solution)/shard_map/all_to_all | solution.py:62
  382.3 291.5 %reduce-scatter.2.cloned.1.call-start = ((), (), s32[]{:S(2)}) async-start(), calls=%async_computation.5 | async-start | bytes 9437184 | tf_op jit(solution)/shard_map/reduce_scatter | solution.py:66
Sparse Core Ops, SparseCore 0:
  9.1 53.5 all-gather.1
  616.1 57.6 reduce-scatter.1
